TPU v7x, 32 devices: a whole 2x2x4 slice. The times are simulated.
32 devices in a mesh: groups: 2 (over y), tile: 8 (over z, x), col: 2 (over core).
Axes of the slice: x: 2, y: 2, z: 4, core: 2. Of those that a mesh axis runs over, the one named last changes fastest.
Arguments:
- jacobian: bfloat16 [512, 3, 128, 512], P(('groups', 'tile'), None, None, 'col'), parts along dimension 0, may hold values from -0.15625 to 0.15625
- footprint: int32 [512, 3], P(('groups', 'tile')), parts along dimension 0, may hold values from 0 to 4, all different within a row
- live: int32 [16], P(('groups', 'tile')), parts along dimension 0, may hold values from 1 to 32, as said below
- noise_weight: float32 [512, 128], P(('groups', 'tile')), parts along dimension 0, may hold values from 0.25 to 4
- probes: bfloat16 [16, 512, 256], P(('groups', 'tile'), 'col'), parts along dimension 0, may hold values from -6 to 6
Outputs:
- basis: float32 [16, 512, 256], P(('groups', 'tile'), 'col'), parts along dimension 0
- factor: float32 [512, 256], P('groups'), parts along dimension 0
There are 2 independent parts, one for each index of `groups`. A program takes and returns all parts, laid end to end along the dimension named above; each array names one. Nothing has to cross between parts.
Inputs may be any that keep to these rules, and one draw needn't show every extreme that they name: `footprint`: each row lists 3 different offsets. Some band has all 32 slots live.
All inputs are finite; a program needn't handle non-finite values.
Results may differ from a plain program's by a relative error of at most 0.0014.
Values may be sent and summed in bfloat16 or wider, within the bound.
A program may use at most 64 MiB of HBM per device.

v0:
```python
import math
import jax
import jax.numpy as jnp
from jax import lax
from jax.sharding import PartitionSpec as P


def shifted(value, axis, steps):
    count = lax.axis_size(axis)
    pairs = [(source, (source + steps) % count) for source in range(count)]
    return lax.ppermute(value, axis, pairs)


def neighbour(piece, offset):
    return shifted(piece, "tile", offset)


def on_device(jacobian, footprint, live, noise_weight, probes):
    slots, reach, rows, cells = jacobian.shape
    width = probes.shape[2]
    group = math.gcd(slots, 8)
    turns = slots // group
    window = jnp.concatenate(
        [
            neighbour(probes, 2),
            neighbour(probes, 1),
            probes,
            neighbour(probes, -1),
            neighbour(probes, -2),
        ],
        axis=0,
    )
    onehot = footprint[:, :, None] == jnp.arange(5, dtype=jnp.int32)[None, None, :]
    hot_narrow = onehot.astype(jnp.bfloat16).reshape(turns, group, reach, 5)
    hot_wide = onehot.astype(jnp.float32).reshape(turns, group, reach, 5)
    jac_groups = jacobian.reshape(turns, group, reach, rows, cells)

    def forward(carry, inputs):
        jac_part, hot_part = inputs
        picked = jnp.einsum(
            "gfo,ock->gfck", hot_part, window, preferred_element_type=jnp.float32
        ).astype(jnp.bfloat16)
        images = jnp.einsum("gfrc,gfck->grk", jac_part, picked, preferred_element_type=jnp.float32)
        return (carry, images)

    _, partial_value = lax.scan(forward, jnp.zeros((), jnp.float32), (jac_groups, hot_narrow))
    partial_value = partial_value.reshape(slots, rows, width)
    active = (jnp.arange(slots, dtype=jnp.int32) < live[0]).astype(jnp.float32)
    scaling = noise_weight * active[:, None]
    share = lax.psum_scatter(partial_value, "col", scatter_dimension=1, tiled=True)
    half = share.shape[1]
    local_scale = lax.dynamic_slice_in_dim(scaling, lax.axis_index("col") * half, half, 1)
    piece = (share * local_scale[:, :, None]).astype(jnp.bfloat16)
    weighted = lax.all_gather(piece, "col", axis=1, tiled=True)
    weighted_groups = weighted.reshape(turns, group, rows, width)

    def backward(bucket, inputs):
        jac_part, hot_part, weighted_part = inputs
        contrib = jnp.einsum(
            "gfrc,grk->gfck", jac_part, weighted_part, preferred_element_type=jnp.float32
        )
        added = jnp.einsum("gfo,gfck->ock", hot_part, contrib, precision=lax.Precision.HIGHEST)
        return (bucket + added, None)

    bucket, _ = lax.scan(
        backward, jnp.zeros((5, cells, width), jnp.float32), (jac_groups, hot_wide, weighted_groups)
    )
    total = bucket[2]
    for offset in (-2, -1, 1, 2):
        total = total + shifted(bucket[2 + offset], "tile", offset)
    field = probes[0].astype(jnp.float32) + total
    local_gram = jnp.dot(field.T, field, precision=lax.Precision.HIGHEST)
    gram = lax.psum(local_gram, ("tile", "col"))
    lower = jnp.linalg.cholesky(gram)
    states = cells * lax.axis_size("col") * lax.axis_size("tile")
    scale = math.sqrt(states)
    solved = jax.scipy.linalg.solve_triangular(lower, field.T, lower=True)
    basis = (solved.T * scale)[None]
    factor = lower.T / scale
    return (basis, factor)


def solution(mesh):
    placed = (
        P(("groups", "tile"), None, None, "col"),
        P(("groups", "tile"), None),
        P(("groups", "tile")),
        P(("groups", "tile"), None),
        P(("groups", "tile"), "col", None),
    )
    return jax.shard_map(
        on_device,
        mesh=mesh,
        in_specs=placed,
        out_specs=(P(("groups", "tile"), "col", None), P("groups", None)),
        check_vma=False,
    )
```

profile of v0, /device:TPU:0, one launch (start us, length us, event | category | flops | bytes accessed | tf_op | source)
XLA Modules:
  0.0 315.2 jit_solution(8248134718715111169)
XLA Ops:
  7.2 3.1 collective-permute-start
  10.3 1.5 collective-permute-start.1
  11.8 3.2 %collective-permute-start.2 = (bf16[1,256,256]{2,1,0:T(8,128)(2,1)}, bf16[1,256,256]{2,1,0:T(8,128)(2,1)S(1)}, u32[]{:S(2)}, u32[]{:S(2)}) collective-permute-start(bf16[1,256,256]{2,1,0:T(8,128)(2,1)} %param.13), channel_id=1, source_target_pairs={{0,14},{2,0},{4,2},{6,4},{8,6},{10,8},{12,10},{14,12},{1,15},{3,1}... | collective-permute-start | bytes 393224 | tf_op jit(solution)/shard_map/ppermute | solution.py:11
  15.3 0.8 eq.17
  16.4 4.4 %collective-permute-done.1 = bf16[1,256,256]{2,1,0:T(8,128)(2,1)S(1)} collective-permute-done((bf16[1,256,256]{2,1,0:T(8,128)(2,1)}, bf16[1,256,256]{2,1,0:T(8,128)(2,1)S(1)}, u32[]{:S(2)}, u32[]{:S(2)}) %collective-permute-start.1) | collective-permute-done | bytes 131104 | tf_op jit(solution)/shard_map/ppermute | solution.py:11
  20.9 0.9 constant_dynamic-update-slice_fusion.2
  21.9 17.7 %while.22 = (s32[]{:T(128)}, f32[4,8,128,256]{3,2,1,0:T(8,128)}, bf16[4,8,3,128,256]{4,3,2,1,0:T(8,128)(2,1)}, bf16[4,8,3,5]{1,2,3,0:T(4,128)(2,1)S(1)}, bf16[5,256,256]{2,1,0:T(8,128)(2,1)S(1)}, /*index=5*/s32[]{:T(128)}) while((s32[]{:T(128)}, f32[4,8,128,256]{3,2,1,0:T(8,128)}, bf16[4,8,3,128,256]{4,3,2,1,0:T(8,128)(2,1)}, ...), condition=%wide.region_1.2_spmd, body=%wide.region_0.1_spmd.sunk | while | flops 418381824 | bytes 9570073 | solution.py:46
  21.9 1.3 fusion.64
  23.2 3.1 fusion.65
  26.3 1.3 fusion.64
  27.6 3.1 fusion.65
  30.7 1.3 fusion.64
  32.0 3.1 fusion.65
  35.1 1.3 fusion.64
  36.4 3.1 fusion.65
  40.4 11.5 %reduce-scatter.2.cloned.1.call-done = f32[32,64,256]{2,1,0:T(8,128)} async-done(((f32[32,128,256]{2,1,0:T(8,128)}), f32[32,64,256]{2,1,0:T(8,128)}) %reduce-scatter.2.cloned.1.call-update) | async-done | bytes 2097168 | tf_op jit(solution)/shard_map/reduce_scatter | solution.py:50
  51.8 2.9 multiply_convert_fusion
  54.8 11.9 %all-gather.2.cloned.1.call-done = bf16[32,128,256]{2,1,0:T(8,128)(2,1)} async-done(((bf16[32,64,256]{2,1,0:T(8,128)(2,1)}), bf16[32,128,256]{2,1,0:T(8,128)(2,1)}) %all-gather.2.cloned.1.call-update) | async-done | bytes 2097168 | tf_op jit(solution)/shard_map/all_gather | solution.py:54
  66.8 62.4 %while.24 = (s32[]{:T(128)}, f32[5,256,256]{2,0,1:T(8,128)S(1)}, f32[4,8,3,5]{1,2,3,0:T(4,128)S(1)}, bf16[4,8,3,128,256]{4,3,2,1,0:T(8,128)(2,1)}, bf16[4,8,128,256]{3,2,1,0:T(8,128)(2,1)}, /*index=5*/s32[]{:T(128)}, s32[]{:T(128)}) while((s32[]{:T(128)}, f32[5,256,256]{2,0,1:T(8,128)S(1)}, f32[4,8,3,5]{1,2,3,0:T(4,128)S(1)}, ...), condition=%wide.region_4.5_spmd.clone, body=%wide.region_3.4_spmd.clone.sunk | while | flops 497680384 | bytes 17304060 | solution.py:65
  66.8 5.2 %fusion.71 = f32[8,3,256,256]{3,2,1,0:T(8,128)} fusion(bf16[4,8,3,128,256]{4,3,2,1,0:T(8,128)(2,1)} %get-tuple-element.257, s32[]{:T(128)} %get-tuple-element.247, bf16[4,8,128,256]{3,2,1,0:T(8,128)(2,1)} %get-tuple-element.258), kind=kOutput, calls=%fused_computation.16.clone.1 | convolution fusion | flops 402653184 | bytes 8389632 | tf_op jit(solution)/shard_map/while/body/eval_jaxpr/gfrc,grk->gfck/dot_general | solution.py:59
  72.0 10.4 %bitcast_add_fusion.3 = f32[5,256,256]{2,0,1:T(8,128)S(1)} fusion(f32[5,256,256]{2,0,1:T(8,128)S(1)} %get-tuple-element.248, f32[8,3,256,256]{3,2,1,0:T(8,128)} %fusion.71, pred[]{:T(512)S(6)} %compare.27, f32[8,3,5]{0,1,2:T(4,128)S(1)} %dynamic-slice_bitcast_fusion.5), kind=kOutput, calls=%fused_computation.15.clone.1 | convolution fusion | flops 95027200 | bytes 8913377 | tf_op jit(solution)/shard_map/while/body/eval_jaxpr/gfo,gfck->ock/dot_general | solution.py:62
  82.4 5.2 %fusion.71 = f32[8,3,256,256]{3,2,1,0:T(8,128)} fusion(bf16[4,8,3,128,256]{4,3,2,1,0:T(8,128)(2,1)} %get-tuple-element.257, s32[]{:T(128)} %get-tuple-element.247, bf16[4,8,128,256]{3,2,1,0:T(8,128)(2,1)} %get-tuple-element.258), kind=kOutput, calls=%fused_computation.16.clone.1 | convolution fusion | flops 402653184 | bytes 8389632 | tf_op jit(solution)/shard_map/while/body/eval_jaxpr/gfrc,grk->gfck/dot_general | solution.py:59
  87.6 10.4 %bitcast_add_fusion.3 = f32[5,256,256]{2,0,1:T(8,128)S(1)} fusion(f32[5,256,256]{2,0,1:T(8,128)S(1)} %get-tuple-element.248, f32[8,3,256,256]{3,2,1,0:T(8,128)} %fusion.71, pred[]{:T(512)S(6)} %compare.27, f32[8,3,5]{0,1,2:T(4,128)S(1)} %dynamic-slice_bitcast_fusion.5), kind=kOutput, calls=%fused_computation.15.clone.1 | convolution fusion | flops 95027200 | bytes 8913377 | tf_op jit(solution)/shard_map/while/body/eval_jaxpr/gfo,gfck->ock/dot_general | solution.py:62
  97.9 5.2 %fusion.71 = f32[8,3,256,256]{3,2,1,0:T(8,128)} fusion(bf16[4,8,3,128,256]{4,3,2,1,0:T(8,128)(2,1)} %get-tuple-element.257, s32[]{:T(128)} %get-tuple-element.247, bf16[4,8,128,256]{3,2,1,0:T(8,128)(2,1)} %get-tuple-element.258), kind=kOutput, calls=%fused_computation.16.clone.1 | convolution fusion | flops 402653184 | bytes 8389632 | tf_op jit(solution)/shard_map/while/body/eval_jaxpr/gfrc,grk->gfck/dot_general | solution.py:59
  103.2 10.4 %bitcast_add_fusion.3 = f32[5,256,256]{2,0,1:T(8,128)S(1)} fusion(f32[5,256,256]{2,0,1:T(8,128)S(1)} %get-tuple-element.248, f32[8,3,256,256]{3,2,1,0:T(8,128)} %fusion.71, pred[]{:T(512)S(6)} %compare.27, f32[8,3,5]{0,1,2:T(4,128)S(1)} %dynamic-slice_bitcast_fusion.5), kind=kOutput, calls=%fused_computation.15.clone.1 | convolution fusion | flops 95027200 | bytes 8913377 | tf_op jit(solution)/shard_map/while/body/eval_jaxpr/gfo,gfck->ock/dot_general | solution.py:62
  113.5 5.2 %fusion.71 = f32[8,3,256,256]{3,2,1,0:T(8,128)} fusion(bf16[4,8,3,128,256]{4,3,2,1,0:T(8,128)(2,1)} %get-tuple-element.257, s32[]{:T(128)} %get-tuple-element.247, bf16[4,8,128,256]{3,2,1,0:T(8,128)(2,1)} %get-tuple-element.258), kind=kOutput, calls=%fused_computation.16.clone.1 | convolution fusion | flops 402653184 | bytes 8389632 | tf_op jit(solution)/shard_map/while/body/eval_jaxpr/gfrc,grk->gfck/dot_general | solution.py:59
  118.7 10.4 %bitcast_add_fusion.3 = f32[5,256,256]{2,0,1:T(8,128)S(1)} fusion(f32[5,256,256]{2,0,1:T(8,128)S(1)} %get-tuple-element.248, f32[8,3,256,256]{3,2,1,0:T(8,128)} %fusion.71, pred[]{:T(512)S(6)} %compare.27, f32[8,3,5]{0,1,2:T(4,128)S(1)} %dynamic-slice_bitcast_fusion.5), kind=kOutput, calls=%fused_computation.15.clone.1 | convolution fusion | flops 95027200 | bytes 8913377 | tf_op jit(solution)/shard_map/while/body/eval_jaxpr/gfo,gfck->ock/dot_general | solution.py:62
  129.9 3.6 %collective-permute-start.4 = (f32[256,256]{1,0:T(8,128)S(1)}, f32[256,256]{1,0:T(8,128)S(1)}, u32[]{:S(2)}, u32[]{:S(2)}) collective-permute-start(f32[256,256]{1,0:T(8,128)S(1)} %get-tuple-element.116), channel_id=1, source_target_pairs={{0,12},{2,14},{4,0},{6,2},{8,4},{10,6},{12,8},{14,10},{1,13},{3,15... | collective-permute-start | bytes 786440 | tf_op jit(solution)/shard_map/ppermute | solution.py:11
  133.6 1.5 collective-permute-start.6
  135.1 3.5 %collective-permute-start.5 = (f32[256,256]{1,0:T(8,128)S(1)}, f32[256,256]{1,0:T(8,128)S(1)}, u32[]{:S(2)}, u32[]{:S(2)}) collective-permute-start(f32[256,256]{1,0:T(8,128)S(1)} %bitcast.127), channel_id=1, source_target_pairs={{0,14},{2,0},{4,2},{6,4},{8,6},{10,8},{12,10},{14,12},{1,15},{3,1}... | collective-permute-start | bytes 786440 | tf_op jit(solution)/shard_map/ppermute | solution.py:11
  138.5 1.8 collective-permute-done.4
  140.3 7.5 %collective-permute-done.6 = f32[256,256]{1,0:T(8,128)S(1)} collective-permute-done((f32[256,256]{1,0:T(8,128)S(1)}, f32[256,256]{1,0:T(8,128)S(1)}, u32[]{:S(2)}, u32[]{:S(2)}) %collective-permute-start.6) | collective-permute-done | bytes 262176 | tf_op jit(solution)/shard_map/ppermute | solution.py:11
  147.8 3.0 collective-permute-done.5
  151.0 1.3 fusion.44
  152.3 91.8 %all-reduce.3.cloned.1.call-done = f32[256,256]{0,1:T(8,128)} async-done(((f32[256,256]{0,1:T(8,128)}), f32[256,256]{0,1:T(8,128)}) %all-reduce.3.cloned.1.call-update) | async-done | bytes 262160 | tf_op jit(solution)/shard_map/psum | solution.py:73
  244.1 1.1 copy.14
  245.2 1.0 fusion.31
  246.2 11.7 %cholesky.50 = f32[128,128]{1,0:T(8,128)S(1)} custom-call(f32[128,128]{1,0:T(8,128)S(1)} %cholesky.118), custom_call_target="Cholesky" | custom-call | tf_op jit(solution)/shard_map/jit(cholesky)/cholesky | solution.py:74
  258.0 9.8 %custom-call.15 = f32[1,128,128]{1,2,0:T(8,128)S(1)} custom-call(f32[1,128,128]{2,1,0:T(8,128)S(1)} %get-tuple-element.124), custom_call_target="InvertDiagBlocksLowerTriangular" | custom-call | tf_op jit(solution)/shard_map/jit(cholesky)/cholesky | solution.py:74
  268.3 11.7 %cholesky.105 = f32[128,128]{1,0:T(8,128)S(1)} custom-call(f32[128,128]{1,0:T(8,128)S(1)} %convolution_subtract_fusion), custom_call_target="Cholesky" | custom-call | tf_op jit(solution)/shard_map/jit(cholesky)/cholesky | solution.py:74
  280.0 0.7 compare_reduce_fusion
  282.1 4.1 %while.23 = (s32[]{:T(128)}, f32[256,256]{1,0:T(8,128)S(1)}, s32[2,2]{1,0:T(2,128)S(1)}, f32[2,128,128]{2,1,0:T(8,128)S(1)}, s32[]{:T(128)}) while((s32[]{:T(128)}, f32[256,256]{1,0:T(8,128)S(1)}, s32[2,2]{1,0:T(2,128)S(1)}, f32[2,128,128]{2,1,0:T(8,128)S(1)}, s32[]{:T(128)}) %tuple.68), condition=%wide.while_cond, body=%wide.while_body.sunk | while | flops 2 | bytes 131181 | solution.py:77
  282.9 1.4 bitcast_dynamic-update-slice_fusion.2
  284.3 0.6 fusion.66
  284.8 1.4 bitcast_dynamic-update-slice_fusion.2
  286.2 19.7 %custom-call.16 = f32[2,128,128]{1,2,0:T(8,128)S(1)} custom-call(f32[2,128,128]{2,1,0:T(8,128)S(1)} %get-tuple-element.65), custom_call_target="InvertDiagBlocksLowerTriangular" | custom-call | tf_op jit(solution)/shard_map/jit(_solve_triangular)/triangular_solve | solution.py:77
  307.0 0.8 copy.15
  307.8 0.8 copy.16
  (56 shorter events, 4.2 us)
Async XLA Ops:
  7.2 44.7 %reduce-scatter.2.cloned.1.call-start = ((), (), s32[]{:S(2)}) async-start(), calls=%async_computation.1 | async-start | bytes 6291456 | tf_op jit(solution)/shard_map/reduce_scatter | solution.py:50
  7.2 9.2 %collective-permute-start = (bf16[1,256,256]{2,1,0:T(8,128)(2,1)}, bf16[1,256,256]{2,1,0:T(8,128)(2,1)S(1)}, u32[]{:S(2)}, u32[]{:S(2)}) collective-permute-start(bf16[1,256,256]{2,1,0:T(8,128)(2,1)} %param.13), channel_id=1, source_target_pairs={{0,4},{2,6},{4,8},{6,10},{8,12},{10,14},{12,0},{14,2},{1,5},{3,7},... | collective-permute-start | bytes 393224 | tf_op jit(solution)/shard_map/ppermute | solution.py:11
  10.3 10.6 %collective-permute-start.1 = (bf16[1,256,256]{2,1,0:T(8,128)(2,1)}, bf16[1,256,256]{2,1,0:T(8,128)(2,1)S(1)}, u32[]{:S(2)}, u32[]{:S(2)}) collective-permute-start(bf16[1,256,256]{2,1,0:T(8,128)(2,1)} %param.13), channel_id=1, source_target_pairs={{0,2},{2,4},{4,6},{6,8},{8,10},{10,12},{12,14},{14,0},{1,3},{3,5},... | collective-permute-start | bytes 393224 | tf_op jit(solution)/shard_map/ppermute | solution.py:11
  11.8 10.0 %collective-permute-start.2 = (bf16[1,256,256]{2,1,0:T(8,128)(2,1)}, bf16[1,256,256]{2,1,0:T(8,128)(2,1)S(1)}, u32[]{:S(2)}, u32[]{:S(2)}) collective-permute-start(bf16[1,256,256]{2,1,0:T(8,128)(2,1)} %param.13), channel_id=1, source_target_pairs={{0,14},{2,0},{4,2},{6,4},{8,6},{10,8},{12,10},{14,12},{1,15},{3,1}... | collective-permute-start | bytes 393224 | tf_op jit(solution)/shard_map/ppermute | solution.py:11
  15.0 6.8 %collective-permute-start.3 = (bf16[1,256,256]{2,1,0:T(8,128)(2,1)}, bf16[1,256,256]{2,1,0:T(8,128)(2,1)S(1)}, u32[]{:S(2)}, u32[]{:S(2)}) collective-permute-start(bf16[1,256,256]{2,1,0:T(8,128)(2,1)} %param.13), channel_id=1, source_target_pairs={{0,12},{2,14},{4,0},{6,2},{8,4},{10,6},{12,8},{14,10},{1,13},{3,15... | collective-permute-start | bytes 393224 | tf_op jit(solution)/shard_map/ppermute | solution.py:11
  39.5 0.7 copy-start.1
  39.6 27.2 %all-gather.2.cloned.1.call-start = ((), (), s32[]{:S(2)}) async-start(), calls=%async_computation.2 | async-start | bytes 3145728 | tf_op jit(solution)/shard_map/all_gather | solution.py:54
  54.8 189.3 %all-reduce.3.cloned.1.call-start = ((), (), s32[]{:S(2)}) async-start(), calls=%async_computation.3 | async-start | bytes 524288 | tf_op jit(solution)/shard_map/psum | solution.py:73
  129.1 21.7 %copy-start = (bf16[1,256,256]{2,1,0:T(8,128)(2,1)S(1)}, bf16[1,256,256]{2,1,0:T(8,128)(2,1)}, u32[]{:S(2)}) copy-start(bf16[1,256,256]{2,1,0:T(8,128)(2,1)} %param.13) | copy-start | bytes 393220
  129.9 10.4 %collective-permute-start.4 = (f32[256,256]{1,0:T(8,128)S(1)}, f32[256,256]{1,0:T(8,128)S(1)}, u32[]{:S(2)}, u32[]{:S(2)}) collective-permute-start(f32[256,256]{1,0:T(8,128)S(1)} %get-tuple-element.116), channel_id=1, source_target_pairs={{0,12},{2,14},{4,0},{6,2},{8,4},{10,6},{12,8},{14,10},{1,13},{3,15... | collective-permute-start | bytes 786440 | tf_op jit(solution)/shard_map/ppermute | solution.py:11
  133.6 14.2 %collective-permute-start.6 = (f32[256,256]{1,0:T(8,128)S(1)}, f32[256,256]{1,0:T(8,128)S(1)}, u32[]{:S(2)}, u32[]{:S(2)}) collective-permute-start(f32[256,256]{1,0:T(8,128)S(1)} %get-tuple-element.118), channel_id=1, source_target_pairs={{0,2},{2,4},{4,6},{6,8},{8,10},{10,12},{12,14},{14,0},{1,3},{3,5},... | collective-permute-start | bytes 786440 | tf_op jit(solution)/shard_map/ppermute | solution.py:11
  135.0 12.8 %collective-permute-start.7 = (f32[256,256]{1,0:T(8,128)S(1)}, f32[256,256]{1,0:T(8,128)S(1)}, u32[]{:S(2)}, u32[]{:S(2)}) collective-permute-start(f32[256,256]{1,0:T(8,128)S(1)} %get-tuple-element.117), channel_id=1, source_target_pairs={{0,4},{2,6},{4,8},{6,10},{8,12},{10,14},{12,0},{14,2},{1,5},{3,7},... | collective-permute-start | bytes 786440 | tf_op jit(solution)/shard_map/ppermute | solution.py:11
  135.1 15.8 %collective-permute-start.5 = (f32[256,256]{1,0:T(8,128)S(1)}, f32[256,256]{1,0:T(8,128)S(1)}, u32[]{:S(2)}, u32[]{:S(2)}) collective-permute-start(f32[256,256]{1,0:T(8,128)S(1)} %bitcast.127), channel_id=1, source_target_pairs={{0,14},{2,0},{4,2},{6,4},{8,6},{10,8},{12,10},{14,12},{1,15},{3,1}... | collective-permute-start | bytes 786440 | tf_op jit(solution)/shard_map/ppermute | solution.py:11
Sparse Core Ops, SparseCore 0:
  39.7 12.0 reduce-scatter.1
  54.9 11.8 all-gather.1
  152.4 91.6 all-reduce.2
where the time goes:
time: 316 us; the launch traced here: 315 us
  waiting for transfers between devices  132 us (42%)
  matrix products  82.6 us (26%)
  other arithmetic  57.8 us (18%)
  starting transfers between devices  16.9 us (5%)
  between operations  15.9 us (5%)
  local copies, waits for them, and re-layouts  9.31 us (3%)
    psum x1, waiting for transfers between devices, on_device(): gram = lax.psum(local_gram, ('tile', 'col'))  91.8 us
    dot_general x4, matrix products, backward(): jnp.einsum('gfo,gfck->ock', hot_part, contrib, precision=lax.Precision.HI...  41.5 us
    another operation x6, other arithmetic, on_device(): lower = jnp.linalg.cholesky(gram)  34 us
    dot_general x4, matrix products, backward(): jnp.einsum('gfrc,grk->gfck', jac_part, weighted_part, preferred_element_t...  20.8 us
    another operation x2, other arithmetic, on_device(): solved = jax.scipy.linalg.solve_triangular(lower, field.T, lower=True)  19.7 us
    ppermute x8, waiting for transfers between devices, shifted(): return lax.ppermute(value, axis, pairs)  17.1 us
    ppermute x8, starting transfers between devices, shifted(): return lax.ppermute(value, axis, pairs)  16.7 us
    dot_general x4, matrix products, forward(): jnp.einsum('gfrc,gfck->grk', jac_part, picked, preferred_element_type=jnp...  12.5 us
  transfers between devices with their start and end apart: 11, of which 8 were waited for; matrix products, arithmetic and copies ran while one was open for 1% of the time, Pallas kernels for 0%

commit v1 on v0

--- a/solution.py
+++ b/solution.py
@@ -70,7 +70,7 @@
         total = total + shifted(bucket[2 + offset], "tile", offset)
     field = probes[0].astype(jnp.float32) + total
     local_gram = jnp.dot(field.T, field, precision=lax.Precision.HIGHEST)
-    gram = lax.psum(local_gram, ("tile", "col"))
+    gram = jnp.sum(lax.all_gather(local_gram, ("tile", "col")), axis=0)
     lower = jnp.linalg.cholesky(gram)
     states = cells * lax.axis_size("col") * lax.axis_size("tile")
     scale = math.sqrt(states)

time: 316 us -> 277 us (0.88)
  waiting for transfers between devices: 132 us -> 92.9 us
    psum x1 -> x0, waiting for transfers between devices: 91.8 us -> none  [on_device(): gram = lax.psum(local_gram, ('tile', 'col'))]
    all_gather x0 -> x1, waiting for transfers between devices: none -> 52.3 us  [on_device(): gram = jnp.sum(lax.all_gather(local_gram, ('tile', 'col')), axis=0)]
where the time goes in v1:
time: 277 us; the launch traced here: 276 us
  waiting for transfers between devices  92.9 us (34%)
  matrix products  82.6 us (30%)
  other arithmetic  59.3 us (21%)
  starting transfers between devices  16.9 us (6%)
  between operations  15.9 us (6%)
  local copies, waits for them, and re-layouts  8.37 us (3%)
    all_gather x1, waiting for transfers between devices, on_device(): gram = jnp.sum(lax.all_gather(local_gram, ('tile', 'col')), axis=0)  52.3 us
    dot_general x4, matrix products, backward(): jnp.einsum('gfo,gfck->ock', hot_part, contrib, precision=lax.Precision.HI...  41.5 us
    another operation x6, other arithmetic, on_device(): lower = jnp.linalg.cholesky(gram)  34 us
    dot_general x4, matrix products, backward(): jnp.einsum('gfrc,grk->gfck', jac_part, weighted_part, preferred_element_t...  20.8 us
    another operation x2, other arithmetic, on_device(): solved = jax.scipy.linalg.solve_triangular(lower, field.T, lower=True)  19.7 us
    ppermute x8, waiting for transfers between devices, shifted(): return lax.ppermute(value, axis, pairs)  17.1 us
    ppermute x8, starting transfers between devices, shifted(): return lax.ppermute(value, axis, pairs)  16.7 us
    dot_general x4, matrix products, forward(): jnp.einsum('gfrc,gfck->grk', jac_part, picked, preferred_element_type=jnp...  12.5 us
  transfers between devices with their start and end apart: 11, of which 8 were waited for; matrix products, arithmetic and copies ran while one was open for 1% of the time, Pallas kernels for 0%

profile of v1, /device:TPU:0, one launch (start us, length us, event | category | flops | bytes accessed | tf_op | source)
XLA Modules:
  0.0 276.3 jit_solution(12497442744639713552)
XLA Ops:
  7.2 3.1 %collective-permute-start = (bf16[1,256,256]{2,1,0:T(8,128)(2,1)}, bf16[1,256,256]{2,1,0:T(8,128)(2,1)S(1)}, u32[]{:S(2)}, u32[]{:S(2)}) collective-permute-start(bf16[1,256,256]{2,1,0:T(8,128)(2,1)} %param.13), channel_id=1, source_target_pairs={{0,4},{2,6},{4,8},{6,10},{8,12},{10,14},{12,0},{14,2},{1,5},{3,7},... | collective-permute-start | bytes 393224 | tf_op jit(solution)/shard_map/ppermute | solution.py:11
  10.3 1.5 collective-permute-start.1
  11.8 3.2 %collective-permute-start.2 = (bf16[1,256,256]{2,1,0:T(8,128)(2,1)}, bf16[1,256,256]{2,1,0:T(8,128)(2,1)S(1)}, u32[]{:S(2)}, u32[]{:S(2)}) collective-permute-start(bf16[1,256,256]{2,1,0:T(8,128)(2,1)} %param.13), channel_id=1, source_target_pairs={{0,14},{2,0},{4,2},{6,4},{8,6},{10,8},{12,10},{14,12},{1,15},{3,1}... | collective-permute-start | bytes 393224 | tf_op jit(solution)/shard_map/ppermute | solution.py:11
  15.3 0.8 eq.17
  16.4 4.4 %collective-permute-done.1 = bf16[1,256,256]{2,1,0:T(8,128)(2,1)S(1)} collective-permute-done((bf16[1,256,256]{2,1,0:T(8,128)(2,1)}, bf16[1,256,256]{2,1,0:T(8,128)(2,1)S(1)}, u32[]{:S(2)}, u32[]{:S(2)}) %collective-permute-start.1) | collective-permute-done | bytes 131104 | tf_op jit(solution)/shard_map/ppermute | solution.py:11
  20.9 0.9 constant_dynamic-update-slice_fusion.2
  21.9 17.7 %while.22 = (s32[]{:T(128)}, f32[4,8,128,256]{3,2,1,0:T(8,128)}, bf16[4,8,3,128,256]{4,3,2,1,0:T(8,128)(2,1)}, bf16[4,8,3,5]{1,2,3,0:T(4,128)(2,1)S(1)}, bf16[5,256,256]{2,1,0:T(8,128)(2,1)S(1)}, /*index=5*/s32[]{:T(128)}) while((s32[]{:T(128)}, f32[4,8,128,256]{3,2,1,0:T(8,128)}, bf16[4,8,3,128,256]{4,3,2,1,0:T(8,128)(2,1)}, ...), condition=%wide.region_1.2_spmd, body=%wide.region_0.1_spmd.sunk | while | flops 418381824 | bytes 9570073 | solution.py:46
  21.9 1.3 fusion.64
  23.2 3.1 %fusion.65 = f32[4,8,128,256]{3,2,1,0:T(8,128)} fusion(f32[4,8,128,256]{3,2,1,0:T(8,128)} %get-tuple-element.231, s32[]{:T(128)} %get-tuple-element.230, bf16[8,3,256,256]{3,0,2,1:T(8,128)(2,1)S(1)} %fusion.64, bf16[4,8,3,128,256]{4,3,2,1,0:T(8,128)(2,1)} %get-tuple-element.238), kind=kOutput, calls=%fused_computation.5.clone.1 | convolution fusion | flops 402653184 | bytes 5768192 | tf_op jit(solution)/shard_map/while/body/eval_jaxpr/gfrc,gfck->grk/dot_general | solution.py:43
  26.3 1.3 fusion.64
  27.6 3.1 %fusion.65 = f32[4,8,128,256]{3,2,1,0:T(8,128)} fusion(f32[4,8,128,256]{3,2,1,0:T(8,128)} %get-tuple-element.231, s32[]{:T(128)} %get-tuple-element.230, bf16[8,3,256,256]{3,0,2,1:T(8,128)(2,1)S(1)} %fusion.64, bf16[4,8,3,128,256]{4,3,2,1,0:T(8,128)(2,1)} %get-tuple-element.238), kind=kOutput, calls=%fused_computation.5.clone.1 | convolution fusion | flops 402653184 | bytes 5768192 | tf_op jit(solution)/shard_map/while/body/eval_jaxpr/gfrc,gfck->grk/dot_general | solution.py:43
  30.7 1.3 fusion.64
  32.0 3.1 %fusion.65 = f32[4,8,128,256]{3,2,1,0:T(8,128)} fusion(f32[4,8,128,256]{3,2,1,0:T(8,128)} %get-tuple-element.231, s32[]{:T(128)} %get-tuple-element.230, bf16[8,3,256,256]{3,0,2,1:T(8,128)(2,1)S(1)} %fusion.64, bf16[4,8,3,128,256]{4,3,2,1,0:T(8,128)(2,1)} %get-tuple-element.238), kind=kOutput, calls=%fused_computation.5.clone.1 | convolution fusion | flops 402653184 | bytes 5768192 | tf_op jit(solution)/shard_map/while/body/eval_jaxpr/gfrc,gfck->grk/dot_general | solution.py:43
  35.1 1.3 fusion.64
  36.4 3.1 %fusion.65 = f32[4,8,128,256]{3,2,1,0:T(8,128)} fusion(f32[4,8,128,256]{3,2,1,0:T(8,128)} %get-tuple-element.231, s32[]{:T(128)} %get-tuple-element.230, bf16[8,3,256,256]{3,0,2,1:T(8,128)(2,1)S(1)} %fusion.64, bf16[4,8,3,128,256]{4,3,2,1,0:T(8,128)(2,1)} %get-tuple-element.238), kind=kOutput, calls=%fused_computation.5.clone.1 | convolution fusion | flops 402653184 | bytes 5768192 | tf_op jit(solution)/shard_map/while/body/eval_jaxpr/gfrc,gfck->grk/dot_general | solution.py:43
  40.4 11.5 %reduce-scatter.2.cloned.1.call-done = f32[32,64,256]{2,1,0:T(8,128)} async-done(((f32[32,128,256]{2,1,0:T(8,128)}), f32[32,64,256]{2,1,0:T(8,128)}) %reduce-scatter.2.cloned.1.call-update) | async-done | bytes 2097168 | tf_op jit(solution)/shard_map/reduce_scatter | solution.py:50
  51.8 2.9 %multiply_convert_fusion = bf16[32,64,256]{2,1,0:T(8,128)(2,1)} fusion(f32[32,64,256]{2,1,0:T(8,128)} %reduce-scatter.2.cloned.1.call-done, f32[32,64]{1,0:T(8,128)S(1)} %dynamic-slice_multiply_fusion), kind=kLoop, calls=%fused_computation.25 | loop fusion | flops 1048576 | bytes 3153920 | tf_op jit(solution)/shard_map/convert_element_type | solution.py:53
  54.8 11.9 %all-gather.4.cloned.1.call-done = bf16[32,128,256]{2,1,0:T(8,128)(2,1)} async-done(((bf16[32,64,256]{2,1,0:T(8,128)(2,1)}), bf16[32,128,256]{2,1,0:T(8,128)(2,1)}) %all-gather.4.cloned.1.call-update) | async-done | bytes 2097168 | tf_op jit(solution)/shard_map/all_gather | solution.py:54
  66.8 62.4 %while.24 = (s32[]{:T(128)}, f32[5,256,256]{2,0,1:T(8,128)S(1)}, f32[4,8,3,5]{1,2,3,0:T(4,128)S(1)}, bf16[4,8,3,128,256]{4,3,2,1,0:T(8,128)(2,1)}, bf16[4,8,128,256]{3,2,1,0:T(8,128)(2,1)}, /*index=5*/s32[]{:T(128)}, s32[]{:T(128)}) while((s32[]{:T(128)}, f32[5,256,256]{2,0,1:T(8,128)S(1)}, f32[4,8,3,5]{1,2,3,0:T(4,128)S(1)}, ...), condition=%wide.region_4.5_spmd.clone, body=%wide.region_3.4_spmd.clone.sunk | while | flops 497680384 | bytes 17304060 | solution.py:65
  66.8 5.2 %fusion.71 = f32[8,3,256,256]{3,2,1,0:T(8,128)} fusion(bf16[4,8,3,128,256]{4,3,2,1,0:T(8,128)(2,1)} %get-tuple-element.259, s32[]{:T(128)} %get-tuple-element.249, bf16[4,8,128,256]{3,2,1,0:T(8,128)(2,1)} %get-tuple-element.260), kind=kOutput, calls=%fused_computation.16.clone.1 | convolution fusion | flops 402653184 | bytes 8389632 | tf_op jit(solution)/shard_map/while/body/eval_jaxpr/gfrc,grk->gfck/dot_general | solution.py:59
  72.0 10.4 %bitcast_add_fusion.3 = f32[5,256,256]{2,0,1:T(8,128)S(1)} fusion(f32[5,256,256]{2,0,1:T(8,128)S(1)} %get-tuple-element.250, f32[8,3,256,256]{3,2,1,0:T(8,128)} %fusion.71, pred[]{:T(512)S(6)} %compare.27, f32[8,3,5]{0,1,2:T(4,128)S(1)} %dynamic-slice_bitcast_fusion.5), kind=kOutput, calls=%fused_computation.15.clone.1 | convolution fusion | flops 95027200 | bytes 8913377 | tf_op jit(solution)/shard_map/while/body/eval_jaxpr/gfo,gfck->ock/dot_general | solution.py:62
  82.4 5.2 %fusion.71 = f32[8,3,256,256]{3,2,1,0:T(8,128)} fusion(bf16[4,8,3,128,256]{4,3,2,1,0:T(8,128)(2,1)} %get-tuple-element.259, s32[]{:T(128)} %get-tuple-element.249, bf16[4,8,128,256]{3,2,1,0:T(8,128)(2,1)} %get-tuple-element.260), kind=kOutput, calls=%fused_computation.16.clone.1 | convolution fusion | flops 402653184 | bytes 8389632 | tf_op jit(solution)/shard_map/while/body/eval_jaxpr/gfrc,grk->gfck/dot_general | solution.py:59
  87.6 10.4 %bitcast_add_fusion.3 = f32[5,256,256]{2,0,1:T(8,128)S(1)} fusion(f32[5,256,256]{2,0,1:T(8,128)S(1)} %get-tuple-element.250, f32[8,3,256,256]{3,2,1,0:T(8,128)} %fusion.71, pred[]{:T(512)S(6)} %compare.27, f32[8,3,5]{0,1,2:T(4,128)S(1)} %dynamic-slice_bitcast_fusion.5), kind=kOutput, calls=%fused_computation.15.clone.1 | convolution fusion | flops 95027200 | bytes 8913377 | tf_op jit(solution)/shard_map/while/body/eval_jaxpr/gfo,gfck->ock/dot_general | solution.py:62
  97.9 5.2 %fusion.71 = f32[8,3,256,256]{3,2,1,0:T(8,128)} fusion(bf16[4,8,3,128,256]{4,3,2,1,0:T(8,128)(2,1)} %get-tuple-element.259, s32[]{:T(128)} %get-tuple-element.249, bf16[4,8,128,256]{3,2,1,0:T(8,128)(2,1)} %get-tuple-element.260), kind=kOutput, calls=%fused_computation.16.clone.1 | convolution fusion | flops 402653184 | bytes 8389632 | tf_op jit(solution)/shard_map/while/body/eval_jaxpr/gfrc,grk->gfck/dot_general | solution.py:59
  103.2 10.4 %bitcast_add_fusion.3 = f32[5,256,256]{2,0,1:T(8,128)S(1)} fusion(f32[5,256,256]{2,0,1:T(8,128)S(1)} %get-tuple-element.250, f32[8,3,256,256]{3,2,1,0:T(8,128)} %fusion.71, pred[]{:T(512)S(6)} %compare.27, f32[8,3,5]{0,1,2:T(4,128)S(1)} %dynamic-slice_bitcast_fusion.5), kind=kOutput, calls=%fused_computation.15.clone.1 | convolution fusion | flops 95027200 | bytes 8913377 | tf_op jit(solution)/shard_map/while/body/eval_jaxpr/gfo,gfck->ock/dot_general | solution.py:62
  113.5 5.2 %fusion.71 = f32[8,3,256,256]{3,2,1,0:T(8,128)} fusion(bf16[4,8,3,128,256]{4,3,2,1,0:T(8,128)(2,1)} %get-tuple-element.259, s32[]{:T(128)} %get-tuple-element.249, bf16[4,8,128,256]{3,2,1,0:T(8,128)(2,1)} %get-tuple-element.260), kind=kOutput, calls=%fused_computation.16.clone.1 | convolution fusion | flops 402653184 | bytes 8389632 | tf_op jit(solution)/shard_map/while/body/eval_jaxpr/gfrc,grk->gfck/dot_general | solution.py:59
  118.7 10.4 %bitcast_add_fusion.3 = f32[5,256,256]{2,0,1:T(8,128)S(1)} fusion(f32[5,256,256]{2,0,1:T(8,128)S(1)} %get-tuple-element.250, f32[8,3,256,256]{3,2,1,0:T(8,128)} %fusion.71, pred[]{:T(512)S(6)} %compare.27, f32[8,3,5]{0,1,2:T(4,128)S(1)} %dynamic-slice_bitcast_fusion.5), kind=kOutput, calls=%fused_computation.15.clone.1 | convolution fusion | flops 95027200 | bytes 8913377 | tf_op jit(solution)/shard_map/while/body/eval_jaxpr/gfo,gfck->ock/dot_general | solution.py:62
  129.9 3.6 %collective-permute-start.4 = (f32[256,256]{1,0:T(8,128)S(1)}, f32[256,256]{1,0:T(8,128)S(1)}, u32[]{:S(2)}, u32[]{:S(2)}) collective-permute-start(f32[256,256]{1,0:T(8,128)S(1)} %get-tuple-element.118), channel_id=1, source_target_pairs={{0,12},{2,14},{4,0},{6,2},{8,4},{10,6},{12,8},{14,10},{1,13},{3,15... | collective-permute-start | bytes 786440 | tf_op jit(solution)/shard_map/ppermute | solution.py:11
  133.6 1.5 collective-permute-start.6
  135.1 3.5 %collective-permute-start.5 = (f32[256,256]{1,0:T(8,128)S(1)}, f32[256,256]{1,0:T(8,128)S(1)}, u32[]{:S(2)}, u32[]{:S(2)}) collective-permute-start(f32[256,256]{1,0:T(8,128)S(1)} %bitcast.129), channel_id=1, source_target_pairs={{0,14},{2,0},{4,2},{6,4},{8,6},{10,8},{12,10},{14,12},{1,15},{3,1}... | collective-permute-start | bytes 786440 | tf_op jit(solution)/shard_map/ppermute | solution.py:11
  138.5 1.8 collective-permute-done.4
  140.3 7.5 %collective-permute-done.6 = f32[256,256]{1,0:T(8,128)S(1)} collective-permute-done((f32[256,256]{1,0:T(8,128)S(1)}, f32[256,256]{1,0:T(8,128)S(1)}, u32[]{:S(2)}, u32[]{:S(2)}) %collective-permute-start.6) | collective-permute-done | bytes 262176 | tf_op jit(solution)/shard_map/ppermute | solution.py:11
  147.8 3.0 %collective-permute-done.5 = f32[256,256]{1,0:T(8,128)S(1)} collective-permute-done((f32[256,256]{1,0:T(8,128)S(1)}, f32[256,256]{1,0:T(8,128)S(1)}, u32[]{:S(2)}, u32[]{:S(2)}) %collective-permute-start.5) | collective-permute-done | bytes 262176 | tf_op jit(solution)/shard_map/ppermute | solution.py:11
  151.0 1.3 fusion.44
  152.3 52.3 %all-gather.6.cloned.1.call-done = f32[4096,256]{1,0:T(8,128)} async-done(((f32[256,256]{1,0:T(8,128)}), f32[4096,256]{1,0:T(8,128)}) %all-gather.6.cloned.1.call-update) | async-done | bytes 4194320 | tf_op jit(solution)/shard_map/all_gather | solution.py:73
  204.7 2.5 reduce_sum.9
  207.3 11.7 %cholesky.50 = f32[128,128]{1,0:T(8,128)S(1)} custom-call(f32[128,128]{1,0:T(8,128)S(1)} %cholesky.118), custom_call_target="Cholesky" | custom-call | tf_op jit(solution)/shard_map/jit(cholesky)/cholesky | solution.py:74
  219.1 9.8 %custom-call.15 = f32[1,128,128]{1,2,0:T(8,128)S(1)} custom-call(f32[1,128,128]{2,1,0:T(8,128)S(1)} %get-tuple-element.126), custom_call_target="InvertDiagBlocksLowerTriangular" | custom-call | tf_op jit(solution)/shard_map/jit(cholesky)/cholesky | solution.py:74
  229.4 11.7 %cholesky.105 = f32[128,128]{1,0:T(8,128)S(1)} custom-call(f32[128,128]{1,0:T(8,128)S(1)} %convolution_subtract_fusion), custom_call_target="Cholesky" | custom-call | tf_op jit(solution)/shard_map/jit(cholesky)/cholesky | solution.py:74
  241.2 0.7 compare_reduce_fusion
  243.2 4.1 %while.23 = (s32[]{:T(128)}, f32[256,256]{1,0:T(8,128)S(1)}, s32[2,2]{1,0:T(2,128)S(1)}, f32[2,128,128]{2,1,0:T(8,128)S(1)}, s32[]{:T(128)}) while((s32[]{:T(128)}, f32[256,256]{1,0:T(8,128)S(1)}, s32[2,2]{1,0:T(2,128)S(1)}, f32[2,128,128]{2,1,0:T(8,128)S(1)}, s32[]{:T(128)}) %tuple.69), condition=%wide.while_cond, body=%wide.while_body.sunk | while | flops 2 | bytes 131181 | solution.py:77
  243.4 0.6 fusion.66
  244.0 1.4 bitcast_dynamic-update-slice_fusion.2
  245.4 0.6 fusion.66
  246.0 1.4 bitcast_dynamic-update-slice_fusion.2
  247.4 19.7 %custom-call.16 = f32[2,128,128]{1,2,0:T(8,128)S(1)} custom-call(f32[2,128,128]{2,1,0:T(8,128)S(1)} %get-tuple-element.65), custom_call_target="InvertDiagBlocksLowerTriangular" | custom-call | tf_op jit(solution)/shard_map/jit(_solve_triangular)/triangular_solve | solution.py:77
  268.1 0.8 copy.23
  269.0 0.8 copy.24
  (57 shorter events, 3.7 us)
Async XLA Ops:
  7.2 44.7 %reduce-scatter.2.cloned.1.call-start = ((), (), s32[]{:S(2)}) async-start(), calls=%async_computation.1 | async-start | bytes 6291456 | tf_op jit(solution)/shard_map/reduce_scatter | solution.py:50
  7.2 9.2 %collective-permute-start = (bf16[1,256,256]{2,1,0:T(8,128)(2,1)}, bf16[1,256,256]{2,1,0:T(8,128)(2,1)S(1)}, u32[]{:S(2)}, u32[]{:S(2)}) collective-permute-start(bf16[1,256,256]{2,1,0:T(8,128)(2,1)} %param.13), channel_id=1, source_target_pairs={{0,4},{2,6},{4,8},{6,10},{8,12},{10,14},{12,0},{14,2},{1,5},{3,7},... | collective-permute-start | bytes 393224 | tf_op jit(solution)/shard_map/ppermute | solution.py:11
  10.3 10.6 %collective-permute-start.1 = (bf16[1,256,256]{2,1,0:T(8,128)(2,1)}, bf16[1,256,256]{2,1,0:T(8,128)(2,1)S(1)}, u32[]{:S(2)}, u32[]{:S(2)}) collective-permute-start(bf16[1,256,256]{2,1,0:T(8,128)(2,1)} %param.13), channel_id=1, source_target_pairs={{0,2},{2,4},{4,6},{6,8},{8,10},{10,12},{12,14},{14,0},{1,3},{3,5},... | collective-permute-start | bytes 393224 | tf_op jit(solution)/shard_map/ppermute | solution.py:11
  11.8 10.0 %collective-permute-start.2 = (bf16[1,256,256]{2,1,0:T(8,128)(2,1)}, bf16[1,256,256]{2,1,0:T(8,128)(2,1)S(1)}, u32[]{:S(2)}, u32[]{:S(2)}) collective-permute-start(bf16[1,256,256]{2,1,0:T(8,128)(2,1)} %param.13), channel_id=1, source_target_pairs={{0,14},{2,0},{4,2},{6,4},{8,6},{10,8},{12,10},{14,12},{1,15},{3,1}... | collective-permute-start | bytes 393224 | tf_op jit(solution)/shard_map/ppermute | solution.py:11
  15.0 6.8 %collective-permute-start.3 = (bf16[1,256,256]{2,1,0:T(8,128)(2,1)}, bf16[1,256,256]{2,1,0:T(8,128)(2,1)S(1)}, u32[]{:S(2)}, u32[]{:S(2)}) collective-permute-start(bf16[1,256,256]{2,1,0:T(8,128)(2,1)} %param.13), channel_id=1, source_target_pairs={{0,12},{2,14},{4,0},{6,2},{8,4},{10,6},{12,8},{14,10},{1,13},{3,15... | collective-permute-start | bytes 393224 | tf_op jit(solution)/shard_map/ppermute | solution.py:11
  39.5 0.7 copy-start.1
  39.6 27.2 %all-gather.4.cloned.1.call-start = ((), (), s32[]{:S(2)}) async-start(), calls=%async_computation.2 | async-start | bytes 3145728 | tf_op jit(solution)/shard_map/all_gather | solution.py:54
  54.8 149.9 %all-gather.6.cloned.1.call-start = ((), (), s32[]{:S(2)}) async-start(), calls=%async_computation.3 | async-start | bytes 4456448 | tf_op jit(solution)/shard_map/all_gather | solution.py:73
  129.1 21.7 %copy-start = (bf16[1,256,256]{2,1,0:T(8,128)(2,1)S(1)}, bf16[1,256,256]{2,1,0:T(8,128)(2,1)}, u32[]{:S(2)}) copy-start(bf16[1,256,256]{2,1,0:T(8,128)(2,1)} %param.13) | copy-start | bytes 393220
  129.9 10.4 %collective-permute-start.4 = (f32[256,256]{1,0:T(8,128)S(1)}, f32[256,256]{1,0:T(8,128)S(1)}, u32[]{:S(2)}, u32[]{:S(2)}) collective-permute-start(f32[256,256]{1,0:T(8,128)S(1)} %get-tuple-element.118), channel_id=1, source_target_pairs={{0,12},{2,14},{4,0},{6,2},{8,4},{10,6},{12,8},{14,10},{1,13},{3,15... | collective-permute-start | bytes 786440 | tf_op jit(solution)/shard_map/ppermute | solution.py:11
  133.6 14.2 %collective-permute-start.6 = (f32[256,256]{1,0:T(8,128)S(1)}, f32[256,256]{1,0:T(8,128)S(1)}, u32[]{:S(2)}, u32[]{:S(2)}) collective-permute-start(f32[256,256]{1,0:T(8,128)S(1)} %get-tuple-element.120), channel_id=1, source_target_pairs={{0,2},{2,4},{4,6},{6,8},{8,10},{10,12},{12,14},{14,0},{1,3},{3,5},... | collective-permute-start | bytes 786440 | tf_op jit(solution)/shard_map/ppermute | solution.py:11
  135.0 12.8 %collective-permute-start.7 = (f32[256,256]{1,0:T(8,128)S(1)}, f32[256,256]{1,0:T(8,128)S(1)}, u32[]{:S(2)}, u32[]{:S(2)}) collective-permute-start(f32[256,256]{1,0:T(8,128)S(1)} %get-tuple-element.119), channel_id=1, source_target_pairs={{0,4},{2,6},{4,8},{6,10},{8,12},{10,14},{12,0},{14,2},{1,5},{3,7},... | collective-permute-start | bytes 786440 | tf_op jit(solution)/shard_map/ppermute | solution.py:11
  135.1 15.8 %collective-permute-start.5 = (f32[256,256]{1,0:T(8,128)S(1)}, f32[256,256]{1,0:T(8,128)S(1)}, u32[]{:S(2)}, u32[]{:S(2)}) collective-permute-start(f32[256,256]{1,0:T(8,128)S(1)} %bitcast.129), channel_id=1, source_target_pairs={{0,14},{2,0},{4,2},{6,4},{8,6},{10,8},{12,10},{14,12},{1,15},{3,1}... | collective-permute-start | bytes 786440 | tf_op jit(solution)/shard_map/ppermute | solution.py:11
Sparse Core Ops, SparseCore 0:
  39.7 12.0 reduce-scatter.1
  54.9 11.8 all-gather.3
  152.4 52.2 all-gather.5
